TPU v7x, 512 devices: a whole 4x8x8 slice. The times are simulated.
512 devices in a mesh: outer: 2 (over core), row: 256 (over y, z, x).
Axes of the slice: x: 4, y: 8, z: 8, core: 2. Of those that a mesh axis runs over, the one named last changes fastest.
Arguments:
- grad_gate: bfloat16 [2, 8192, 14336], P('outer', 'row'), may hold values from -24 to 24
- grad_up: bfloat16 [2, 8192, 14336], P('outer', 'row'), may hold values from -24 to 24
- basis_gate: bfloat16 [32, 14336], P(None, 'row'), may hold values from -0.046875 to 0.046875
- basis_up: bfloat16 [32, 14336], P(None, 'row'), may hold values from -0.046875 to 0.046875
Outputs:
- next_gate: float32 [32, 14336], P(None, 'row')
- next_up: float32 [32, 14336], P(None, 'row')
- factor_gate: float32 [8192, 32], P('row')
- factor_up: float32 [8192, 32], P('row')
- resid_gate: bfloat16 [2, 8192, 14336], P('outer', 'row')
- resid_up: bfloat16 [2, 8192, 14336], P('outer', 'row')
All inputs are finite; a program needn't handle non-finite values.
Results may differ from a plain program's by a relative error of at most 0.005.
Values may be sent and summed in bfloat16 or wider, within the bound.
No kernel may reach another device: no remote copies, remote signals or barrier semaphores. Data moves between devices by JAX's collectives and lax.ppermute only.
A program may use at most 64 MiB of HBM per device.

v0:
```python
import jax
import jax.numpy as jnp
from jax import lax
from jax.sharding import Mesh
from jax.sharding import PartitionSpec as P

ROW = ("row_0", "row_1", "row_2")
OUTER_ROW = ("outer", "row_0", "row_1", "row_2")


def gather_turned(arrays, axis, dims):
    turned = [jnp.moveaxis(a, dim, 0) for a, dim in zip(arrays, dims)]
    widths = [t[0].size for t in turned]
    both = jnp.concatenate([t.reshape(-1, w) for t, w in zip(turned, widths)], axis=1)
    out = lax.all_gather(both, axis, axis=0, tiled=True)
    tiles = jnp.split(out, [sum(widths[:k]) for k in range(1, len(widths))], axis=1)
    return tuple(
        (
            jnp.moveaxis(b.reshape(-1, *t.shape[1:]), 0, dim)
            for b, t, dim in zip(tiles, turned, dims)
        )
    )


def copy_for_each(x, axis):
    peers = lax.axis_size(axis)
    return lax.all_to_all(jnp.broadcast_to(x[None], (peers, *x.shape)), axis, 0, 0, tiled=True)


def taken_together(x, axis):
    everything = copy_for_each(x, axis)
    return jnp.sum(everything, axis=0)


def together(arrays, axis):
    line, at, finished = (jnp.concatenate([a.reshape(-1) for a in arrays]), 0, [])
    so_far = taken_together(line, axis)
    for a in arrays:
        finished.append(so_far[at : at + a.size].reshape(a.shape))
        at += a.size
    return tuple(finished)


def over_axes(x, axes):
    for axis in axes:
        x = lax.psum(x, axis)
    return x


def forward_solve(lower_matrix, right_hand):
    return jax.scipy.linalg.solve_triangular(lower_matrix, right_hand, lower=True)


def contract_cols(left, right):
    return lax.dot_general(
        left, right, (((1,), (1,)), ((), ())), preferred_element_type=jnp.float32
    )


def contract_rows(left, right):
    return lax.dot_general(
        left, right, (((0,), (0,)), ((), ())), preferred_element_type=jnp.float32
    )


def local(grad_gate, grad_up, basis_gate, basis_up):
    pod_count = lax.axis_size("outer")
    gate_rows = grad_gate[0]
    up_rows = grad_up[0]
    full_cols = gate_rows.shape[1]
    pieces = gather_turned((basis_gate, basis_up), ROW, (1, 1))
    summed = together(
        (contract_cols(gate_rows, pieces[0]), contract_cols(up_rows, pieces[1])), "outer"
    )
    round_gate = (summed[0] / pod_count).astype(jnp.bfloat16)
    round_up = (summed[1] / pod_count).astype(jnp.bfloat16)
    gram_pair = (
        over_axes(contract_rows(round_gate, round_gate), ROW),
        over_axes(contract_rows(round_up, round_up), ROW),
    )
    lower_gate = jnp.linalg.cholesky(gram_pair[0])
    lower_up = jnp.linalg.cholesky(gram_pair[1])
    products = (contract_rows(round_gate, gate_rows), contract_rows(round_up, up_rows))
    shard_cols = full_cols // lax.axis_size(ROW)
    shard_start = lax.axis_index(ROW) * shard_cols
    totals = lax.psum((products[0], products[1]), OUTER_ROW)
    full_gate = forward_solve(lower_gate, totals[0] / pod_count)
    full_up = forward_solve(lower_up, totals[1] / pod_count)
    next_gate = lax.dynamic_slice_in_dim(full_gate, shard_start, shard_cols, 1)
    next_up = lax.dynamic_slice_in_dim(full_up, shard_start, shard_cols, 1)
    factor_gate = forward_solve(lower_gate, round_gate.astype(jnp.float32).T).T
    factor_up = forward_solve(lower_up, round_up.astype(jnp.float32).T).T
    resid_gate = (
        gate_rows - jnp.dot(factor_gate, full_gate, precision=lax.Precision.HIGHEST)
    ).astype(jnp.bfloat16)
    resid_up = (up_rows - jnp.dot(factor_up, full_up, precision=lax.Precision.HIGHEST)).astype(
        jnp.bfloat16
    )
    return (next_gate, next_up, factor_gate, factor_up, resid_gate[None], resid_up[None])


def solution(mesh):
    finer = Mesh(
        mesh.devices.reshape(mesh.shape["outer"], 8, 8, 4), ("outer", "row_0", "row_1", "row_2")
    )
    placed = (P("outer", ROW, None), P("outer", ROW, None), P(None, ROW), P(None, ROW))
    return jax.shard_map(
        local,
        mesh=finer,
        in_specs=placed,
        out_specs=(
            P(None, ROW),
            P(None, ROW),
            P(ROW, None),
            P(ROW, None),
            P("outer", ROW, None),
            P("outer", ROW, None),
        ),
        check_vma=False,
    )
```

profile of v0, /device:TPU:1, one launch (start us, length us, event | category | flops | bytes accessed | tf_op | source)
XLA Modules:
  0.0 461.2 jit_solution(15747736612643531091)
XLA Ops:
  7.2 0.8 copy.45
  8.0 0.8 copy.44
  8.8 0.7 pad_maximum_fusion
  9.6 131.7 %all-gather.2.cloned.1.call-done = bf16[14336,64]{1,0:T(8,128)(2,1)} async-done(((bf16[56,64]{1,0:T(8,128)(2,1)}), bf16[14336,64]{1,0:T(8,128)(2,1)}) %all-gather.2.cloned.1.call-update) | async-done | bytes 1835024 | tf_op jit(solution)/shard_map/all_gather | solution.py:15
  141.2 4.3 fusion.15
  145.7 3.1 fusion.12
  149.1 8.5 %all_to_all.6 = f32[2,1,2048]{2,1,0:T(1,128)S(1)} all-to-all(f32[2,1,2048]{2,1,0:T(1,128)S(1)} %broadcast_in_dim.7), channel_id=1, replica_groups=mesh['outer'=2,'row_0'=8,'row_1'=8,'row_2'=4] {'outer'}, dimensions={0} | all-to-all | bytes 32768 | tf_op jit(solution)/shard_map/all_to_all | solution.py:27
  157.7 1.7 fusion.21
  159.5 1.7 fusion.18
  161.2 0.2 fusion.44
  161.6 22.9 %all-reduce.2 = (f32[32,32]{0,1:T(8,128)S(1)}, f32[32,32]{0,1:T(8,128)S(1)}) all-reduce(f32[32,32]{0,1:T(8,128)S(1)} %fusion.44, f32[32,32]{0,1:T(8,128)S(1)} %fusion.45), channel_id=1, replica_groups=mesh['outer'=2,'row_0'=8,'row_1'=8,'row_2'=4] {'row_0'}, use_global_device_ids=true, to_apply=%region_1.0 | all-reduce | flops 2048 | bytes 16384 | tf_op jit(solution)/shard_map/psum | solution.py:46
  184.5 22.5 %all-reduce.1 = (f32[32,32]{0,1:T(8,128)S(1)}, f32[32,32]{0,1:T(8,128)S(1)}) all-reduce(f32[32,32]{0,1:T(8,128)S(1)} %get-tuple-element.43, f32[32,32]{0,1:T(8,128)S(1)} %get-tuple-element.44), channel_id=1, replica_groups=mesh['outer'=2,'row_0'=8,'row_1'=8,'row_2'=4] {'row_1'}, use_global_device_ids=true, to_apply=%region_2.0 | all-reduce | flops 2048 | bytes 16384 | tf_op jit(solution)/shard_map/psum | solution.py:46
  207.0 12.3 %all-reduce.3 = (f32[32,32]{0,1:T(8,128)S(1)}, f32[32,32]{0,1:T(8,128)S(1)}) all-reduce(f32[32,32]{0,1:T(8,128)S(1)} %get-tuple-element.41, f32[32,32]{0,1:T(8,128)S(1)} %get-tuple-element.42), channel_id=1, replica_groups=mesh['outer'=2,'row_0'=8,'row_1'=8,'row_2'=4] {'row_2'}, use_global_device_ids=true, to_apply=%region_3.0 | all-reduce | flops 2048 | bytes 16384 | tf_op jit(solution)/shard_map/psum | solution.py:46
  219.4 2.9 cholesky.44
  222.4 0.6 compare_reduce_fusion.1
  223.0 0.7 fusion.26
  223.7 2.4 custom-call.10
  226.1 2.9 cholesky.55
  229.1 0.6 compare_reduce_fusion
  229.7 0.7 fusion.27
  230.4 2.4 custom-call.11
  232.8 0.2 fusion.30
  233.0 0.7 copy.53
  233.7 0.2 fusion.28
  233.9 0.7 copy.54
  234.6 208.2 %all-reduce.6.cloned.1.call-done = (f32[32,14336]{1,0:T(8,128)}, f32[32,14336]{1,0:T(8,128)}) async-done(((f32[32,14336]{1,0:T(8,128)}, f32[32,14336]{1,0:T(8,128)}), (f32[32,14336]{1,0:T(8,128)}, f32[32,14336]{1,0:T(8,128)})) %all-reduce.6.cloned.1.call-update) | async-done | bytes 3670032 | tf_op jit(solution)/shard_map/psum | solution.py:86
  442.9 3.1 fusion.10
  446.0 2.7 fusion.3
  448.7 0.7 constant_dynamic-slice_fusion.1
  449.4 1.6 fusion.8
  451.0 0.7 constant_dynamic-slice_fusion
  451.7 2.6 fusion.2
  (26 shorter events, 1.1 us)
Async XLA Ops:
  7.2 134.1 %all-gather.2.cloned.1.call-start = ((), (), s32[]{:S(2)}) async-start(), calls=%async_computation.1 | async-start | bytes 3684352 | tf_op jit(solution)/shard_map/all_gather | solution.py:15
  9.5 433.4 %all-reduce.6.cloned.1.call-start = ((), (), s32[]{:S(2)}) async-start(), calls=%async_computation.2 | async-start | bytes 7340032 | tf_op jit(solution)/shard_map/psum | solution.py:86
  9.6 136.2 %copy-start = (bf16[1,32,14336]{2,1,0:T(8,128)(2,1)S(1)}, bf16[1,32,14336]{2,1,0:T(8,128)(2,1)}, u32[]{:S(2)}) copy-start(bf16[1,32,14336]{2,1,0:T(8,128)(2,1)} %param.9) | copy-start | bytes 2752516
  148.9 10.6 %copy-start.1 = (bf16[1,32,14336]{2,1,0:T(8,128)(2,1)S(1)}, bf16[1,32,14336]{2,1,0:T(8,128)(2,1)}, u32[]{:S(2)}) copy-start(bf16[1,32,14336]{2,1,0:T(8,128)(2,1)} %param.10) | copy-start | bytes 2752516
  446.0 3.3 copy-start.2
Sparse Core Ops, SparseCore 0:
  13.0 128.2 all-gather.1
  161.3 281.5 all-reduce.5
where the time goes:
time: 462 us; the launch traced here: 461 us
  waiting for transfers between devices  340 us (74%)
  blocking collectives  66.2 us (14%)
  matrix products  21.8 us (5%)
  other arithmetic  14.1 us (3%)
  between operations  14.1 us (3%)
  local copies, waits for them, and re-layouts  4.98 us (1%)
    psum x1, waiting for transfers between devices, local(): totals = lax.psum((products[0], products[1]), OUTER_ROW)  208 us
    all_gather x1, waiting for transfers between devices, gather_turned(): out = lax.all_gather(both, axis, axis=0, tiled=True)  132 us
    psum x3, blocking collectives, over_axes(): x = lax.psum(x, axis)  57.7 us
  transfers between devices with their start and end apart: 2, of which 2 were waited for; matrix products, arithmetic and copies ran while one was open for 3% of the time, Pallas kernels for 0%

commit v1 on v0

--- a/solution.py
+++ b/solution.py
@@ -12,7 +12,9 @@
     turned = [jnp.moveaxis(a, dim, 0) for a, dim in zip(arrays, dims)]
     widths = [t[0].size for t in turned]
     both = jnp.concatenate([t.reshape(-1, w) for t, w in zip(turned, widths)], axis=1)
-    out = lax.all_gather(both, axis, axis=0, tiled=True)
+    out = jnp.concatenate(
+        lax.all_to_all(jnp.stack([both] * lax.axis_size(axis)), axis, 0, 0), axis=0
+    )
     tiles = jnp.split(out, [sum(widths[:k]) for k in range(1, len(widths))], axis=1)
     return tuple(
         (

time: 462 us -> 405 us (0.88)
  waiting for transfers between devices: 340 us -> 253 us
  starting transfers between devices: 0.08 us -> 23.2 us
  local copies, waits for them, and re-layouts: 4.98 us -> 16.3 us
    all_gather x1 -> x0, waiting for transfers between devices: 132 us -> none  [gather_turned(): out = lax.all_gather(both, axis, axis=0, tiled=True)]
    all_to_all x0 -> x1, waiting for transfers between devices: none -> 45.3 us  [gather_turned(): lax.all_to_all(jnp.stack([both] * lax.axis_size(axis)), axis, 0, 0)]
    all_to_all x0 -> x1, starting transfers between devices: none -> 23.2 us  [gather_turned(): lax.all_to_all(jnp.stack([both] * lax.axis_size(axis)), axis, 0, 0)]
    unnamed x10, local copies, waits for them, and re-layouts: 2.99 us -> 11.9 us
  transfers between devices with their start and end apart: 2 -> 2, of which waited for: 2 -> 2; matrix products, arithmetic and copies ran while one was open for 3% -> 4% of each run, Pallas kernels for 0% -> 0%
where the time goes in v1:
time: 405 us
  waiting for transfers between devices  253 us (62%)
  blocking collectives  62.5 us (15%)
  starting transfers between devices  23.2 us (6%)
  matrix products  21.6 us (5%)
  local copies, waits for them, and re-layouts  16.3 us (4%)
  between operations  14.2 us (4%)
  other arithmetic  14.1 us (3%)
    psum x1, waiting for transfers between devices, local(): totals = lax.psum((products[0], products[1]), OUTER_ROW)  207 us
    psum x3, blocking collectives, over_axes(): x = lax.psum(x, axis)  56.2 us
    all_to_all x1, waiting for transfers between devices, gather_turned(): lax.all_to_all(jnp.stack([both] * lax.axis_size(axis)), axis, 0, 0)  45.3 us
    all_to_all x1, starting transfers between devices, gather_turned(): lax.all_to_all(jnp.stack([both] * lax.axis_size(axis)), axis, 0, 0)  23.2 us
    unnamed x10, local copies, waits for them, and re-layouts  11.9 us
  transfers between devices with their start and end apart: 2, of which 2 were waited for; matrix products, arithmetic and copies ran while one was open for 4% of the time, Pallas kernels for 0%

profile of v1, /device:TPU:1, one launch (start us, length us, event | category | flops | bytes accessed | tf_op | source)
XLA Modules:
  0.0 404.5 jit_solution(5068107906102454936)
XLA Ops:
  7.2 0.7 pad_maximum_fusion
  8.0 2.3 stack.2
  10.3 6.9 %reshape.87 = bf16[256,2,1792]{2,1,0:T(2,128)(2,1)} reshape(bf16[256,56,64]{2,1,0:T(8,128)(2,1)} %stack.2) | data formatting | bytes 3670016
  17.1 23.2 %all-to-all-start = ((bf16[256,2,1792]{2,1,0:T(2,128)(2,1)}), bf16[256,2,1792]{2,1,0:T(2,128)(2,1)S(1)}, u32[]{:S(2)}, u32[]{:S(2)}) async-start(bf16[256,2,1792]{2,1,0:T(2,128)(2,1)} %reshape.87), calls=%async_computation | async-start | bytes 3670016 | tf_op jit(solution)/shard_map/all_to_all | solution.py:16
  40.4 45.3 %all-to-all-done = bf16[256,2,1792]{2,1,0:T(2,128)(2,1)S(1)} async-done(((bf16[256,2,1792]{2,1,0:T(2,128)(2,1)}), bf16[256,2,1792]{2,1,0:T(2,128)(2,1)S(1)}, u32[]{:S(2)}, u32[]{:S(2)}) %all-to-all-start) | async-done | bytes 1835040 | tf_op jit(solution)/shard_map/all_to_all | solution.py:16
  85.7 3.6 reshape.88
  89.3 4.2 %fusion.15 = f32[32,32]{0,1:T(8,128)S(1)} fusion(bf16[14336,64]{1,0:T(8,128)(2,1)} %bitcast.67, bf16[1,32,14336]{2,1,0:T(8,128)(2,1)S(1)} %copy-done.1), kind=kOutput, calls=%fused_computation.15 | convolution fusion | flops 29360128 | bytes 2756608 | tf_op jit(solution)/shard_map/dot_general | solution.py:57
  93.6 3.1 fusion.12
  96.9 6.3 %all_to_all.11 = f32[2,1,2048]{2,1,0:T(1,128)S(1)} all-to-all(f32[2,1,2048]{2,1,0:T(1,128)S(1)} %broadcast_in_dim.7), channel_id=1, replica_groups=mesh['outer'=2,'row_0'=8,'row_1'=8,'row_2'=4] {'outer'}, dimensions={0} | all-to-all | bytes 32768 | tf_op jit(solution)/shard_map/all_to_all | solution.py:29
  103.4 1.7 fusion.21
  105.2 1.7 fusion.18
  107.3 22.9 %all-reduce.2 = (f32[32,32]{0,1:T(8,128)S(1)}, f32[32,32]{0,1:T(8,128)S(1)}) all-reduce(f32[32,32]{0,1:T(8,128)S(1)} %fusion.44, f32[32,32]{0,1:T(8,128)S(1)} %fusion.45), channel_id=1, replica_groups=mesh['outer'=2,'row_0'=8,'row_1'=8,'row_2'=4] {'row_0'}, use_global_device_ids=true, to_apply=%region_1.0 | all-reduce | flops 2048 | bytes 16384 | tf_op jit(solution)/shard_map/psum | solution.py:48
  130.2 21.5 %all-reduce.1 = (f32[32,32]{0,1:T(8,128)S(1)}, f32[32,32]{0,1:T(8,128)S(1)}) all-reduce(f32[32,32]{0,1:T(8,128)S(1)} %get-tuple-element.43, f32[32,32]{0,1:T(8,128)S(1)} %get-tuple-element.44), channel_id=1, replica_groups=mesh['outer'=2,'row_0'=8,'row_1'=8,'row_2'=4] {'row_1'}, use_global_device_ids=true, to_apply=%region_2.0 | all-reduce | flops 2048 | bytes 16384 | tf_op jit(solution)/shard_map/psum | solution.py:48
  151.7 11.8 %all-reduce.3 = (f32[32,32]{0,1:T(8,128)S(1)}, f32[32,32]{0,1:T(8,128)S(1)}) all-reduce(f32[32,32]{0,1:T(8,128)S(1)} %get-tuple-element.41, f32[32,32]{0,1:T(8,128)S(1)} %get-tuple-element.42), channel_id=1, replica_groups=mesh['outer'=2,'row_0'=8,'row_1'=8,'row_2'=4] {'row_2'}, use_global_device_ids=true, to_apply=%region_3.0 | all-reduce | flops 2048 | bytes 16384 | tf_op jit(solution)/shard_map/psum | solution.py:48
  163.7 2.9 cholesky.44
  166.6 0.6 compare_reduce_fusion.1
  167.3 0.7 fusion.26
  167.9 2.4 custom-call.10
  170.4 2.9 cholesky.55
  173.3 0.6 compare_reduce_fusion
  174.0 0.7 fusion.27
  174.6 2.4 custom-call.11
  177.1 0.2 fusion.30
  177.3 0.7 copy.51
  178.2 0.7 copy.52
  178.9 207.3 %all-reduce.6.cloned.1.call-done = (f32[32,14336]{1,0:T(8,128)}, f32[32,14336]{1,0:T(8,128)}) async-done(((f32[32,14336]{1,0:T(8,128)}, f32[32,14336]{1,0:T(8,128)}), (f32[32,14336]{1,0:T(8,128)}, f32[32,14336]{1,0:T(8,128)})) %all-reduce.6.cloned.1.call-update) | async-done | bytes 3670032 | tf_op jit(solution)/shard_map/psum | solution.py:88
  386.2 3.1 fusion.10
  389.3 2.7 fusion.3
  392.0 0.7 constant_dynamic-slice_fusion.1
  392.7 1.6 fusion.8
  394.3 0.7 constant_dynamic-slice_fusion
  395.0 2.6 fusion.2
  (27 shorter events, 1.5 us)
Async XLA Ops:
  17.1 68.5 %all-to-all-start = ((bf16[256,2,1792]{2,1,0:T(2,128)(2,1)}), bf16[256,2,1792]{2,1,0:T(2,128)(2,1)S(1)}, u32[]{:S(2)}, u32[]{:S(2)}) async-start(bf16[256,2,1792]{2,1,0:T(2,128)(2,1)} %reshape.87), calls=%async_computation | async-start | bytes 3670016 | tf_op jit(solution)/shard_map/all_to_all | solution.py:16
  40.3 345.9 %all-reduce.6.cloned.1.call-start = ((), (), s32[]{:S(2)}) async-start(), calls=%async_computation.2 | async-start | bytes 7340032 | tf_op jit(solution)/shard_map/psum | solution.py:88
  40.4 48.9 %copy-start.1 = (bf16[1,32,14336]{2,1,0:T(8,128)(2,1)S(1)}, bf16[1,32,14336]{2,1,0:T(8,128)(2,1)}, u32[]{:S(2)}) copy-start(bf16[1,32,14336]{2,1,0:T(8,128)(2,1)} %param.10) | copy-start | bytes 2752516
  89.3 4.3 %copy-start = (bf16[1,32,14336]{2,1,0:T(8,128)(2,1)S(1)}, bf16[1,32,14336]{2,1,0:T(8,128)(2,1)}, u32[]{:S(2)}) copy-start(bf16[1,32,14336]{2,1,0:T(8,128)(2,1)} %param.9) | copy-start | bytes 2752516
  389.3 3.3 copy-start.2
Sparse Core Ops, SparseCore 0:
  107.0 279.1 all-reduce.5

commit v2 on v0

--- a/solution.py
+++ b/solution.py
@@ -43,7 +43,7 @@
 
 def over_axes(x, axes):
     for axis in axes:
-        x = lax.psum(x, axis)
+        x = jnp.sum(lax.all_gather(x, axis), axis=0)
     return x
 
 

time: 462 us -> 525 us (1.14)
  blocking collectives: 66.2 us -> 101 us
  waiting for transfers between devices: 340 us -> 369 us
    all_gather x0 -> x6, blocking collectives: none -> 92.8 us  [over_axes(): x = jnp.sum(lax.all_gather(x, axis), axis=0)]
    psum x3 -> x0, blocking collectives: 57.7 us -> none  [over_axes(): x = lax.psum(x, axis)]
    psum x1, waiting for transfers between devices: 208 us -> 238 us  [local(): totals = lax.psum((products[0], products[1]), OUTER_ROW)]
  transfers between devices with their start and end apart: 2 -> 2, of which waited for: 2 -> 2; matrix products, arithmetic and copies ran while one was open for 3% -> 2% of each run, Pallas kernels for 0% -> 0%
where the time goes in v2:
time: 525 us
  waiting for transfers between devices  369 us (70%)
  blocking collectives  101 us (19%)
  matrix products  22 us (4%)
  other arithmetic  14.2 us (3%)
  between operations  14.2 us (3%)
    psum x1, waiting for transfers between devices, local(): totals = lax.psum((products[0], products[1]), OUTER_ROW)  238 us
    all_gather x1, waiting for transfers between devices, gather_turned(): out = lax.all_gather(both, axis, axis=0, tiled=True)  132 us
    all_gather x6, blocking collectives, over_axes(): x = jnp.sum(lax.all_gather(x, axis), axis=0)  92.8 us
  transfers between devices with their start and end apart: 2, of which 2 were waited for; matrix products, arithmetic and copies ran while one was open for 2% of the time, Pallas kernels for 0%

profile of v2, /device:TPU:1, one launch (start us, length us, event | category | flops | bytes accessed | tf_op | source)
XLA Modules:
  0.0 525.1 jit_solution(14257466853053223523)
XLA Ops:
  7.2 0.8 copy.37
  8.0 0.8 copy.36
  8.8 0.7 pad_maximum_fusion
  9.6 131.7 %all-gather.8.cloned.1.call-done = bf16[14336,64]{1,0:T(8,128)(2,1)} async-done(((bf16[56,64]{1,0:T(8,128)(2,1)}), bf16[14336,64]{1,0:T(8,128)(2,1)}) %all-gather.8.cloned.1.call-update) | async-done | bytes 1835024 | tf_op jit(solution)/shard_map/all_gather | solution.py:15
  141.2 4.3 fusion.15
  145.7 3.2 fusion.12
  149.1 8.4 %all_to_all.6 = f32[2,1,2048]{2,1,0:T(1,128)S(1)} all-to-all(f32[2,1,2048]{2,1,0:T(1,128)S(1)} %broadcast_in_dim.7), channel_id=1, replica_groups=mesh['outer'=2,'row_0'=8,'row_1'=8,'row_2'=4] {'outer'}, dimensions={0} | all-to-all | bytes 32768 | tf_op jit(solution)/shard_map/all_to_all | solution.py:27
  157.7 1.7 fusion.18
  159.6 1.7 fusion.21
  161.3 18.2 %all-gather.3 = f32[256,32]{1,0:T(8,128)S(1)} all-gather(f32[32,32]{1,0:T(8,128)S(1)} %fusion.45), channel_id=5, replica_groups=mesh['outer'=2,'row_0'=8,'row_1'=8,'row_2'=4] {'row_0'}, dimensions={0}, use_global_device_ids=true | all-gather | bytes 36864 | tf_op jit(solution)/shard_map/all_gather | solution.py:46
  179.6 18.2 %all-gather.4 = f32[256,32]{1,0:T(8,128)S(1)} all-gather(f32[32,32]{1,0:T(8,128)S(1)} %reduce_sum.67), channel_id=6, replica_groups=mesh['outer'=2,'row_0'=8,'row_1'=8,'row_2'=4] {'row_1'}, dimensions={0}, use_global_device_ids=true | all-gather | bytes 36864 | tf_op jit(solution)/shard_map/all_gather | solution.py:46
  197.8 9.0 %all-gather.5 = f32[128,32]{1,0:T(8,128)S(1)} all-gather(f32[32,32]{1,0:T(8,128)S(1)} %reduce_sum.68), channel_id=7, replica_groups=mesh['outer'=2,'row_0'=8,'row_1'=8,'row_2'=4] {'row_2'}, dimensions={0}, use_global_device_ids=true | all-gather | bytes 20480 | tf_op jit(solution)/shard_map/all_gather | solution.py:46
  206.9 2.9 cholesky.55
  209.9 0.6 compare_reduce_fusion
  210.5 0.7 fusion.27
  211.2 2.4 custom-call.11
  213.8 18.3 %all-gather = f32[256,32]{1,0:T(8,128)S(1)} all-gather(f32[32,32]{1,0:T(8,128)S(1)} %fusion.44), channel_id=2, replica_groups=mesh['outer'=2,'row_0'=8,'row_1'=8,'row_2'=4] {'row_0'}, dimensions={0}, use_global_device_ids=true | all-gather | bytes 36864 | tf_op jit(solution)/shard_map/all_gather | solution.py:46
  232.1 19.7 %all-gather.1 = f32[256,32]{1,0:T(8,128)S(1)} all-gather(f32[32,32]{1,0:T(8,128)S(1)} %reduce_sum.64), channel_id=3, replica_groups=mesh['outer'=2,'row_0'=8,'row_1'=8,'row_2'=4] {'row_1'}, dimensions={0}, use_global_device_ids=true | all-gather | bytes 36864 | tf_op jit(solution)/shard_map/all_gather | solution.py:46
  251.9 9.3 %all-gather.2 = f32[128,32]{1,0:T(8,128)S(1)} all-gather(f32[32,32]{1,0:T(8,128)S(1)} %reduce_sum.65), channel_id=4, replica_groups=mesh['outer'=2,'row_0'=8,'row_1'=8,'row_2'=4] {'row_2'}, dimensions={0}, use_global_device_ids=true | all-gather | bytes 20480 | tf_op jit(solution)/shard_map/all_gather | solution.py:46
  261.3 2.9 cholesky.44
  264.2 0.6 compare_reduce_fusion.1
  264.9 0.7 fusion.26
  265.5 2.4 custom-call.10
  268.0 0.2 fusion.30
  268.2 0.7 copy.43
  269.1 0.7 copy.44
  269.8 237.5 %all-reduce.3.cloned.1.call-done = (f32[32,14336]{1,0:T(8,128)}, f32[32,14336]{1,0:T(8,128)}) async-done(((f32[32,14336]{1,0:T(8,128)}, f32[32,14336]{1,0:T(8,128)}), (f32[32,14336]{1,0:T(8,128)}, f32[32,14336]{1,0:T(8,128)})) %all-reduce.3.cloned.1.call-update) | async-done | bytes 3670032 | tf_op jit(solution)/shard_map/psum | solution.py:86
  507.3 3.3 fusion.8
  510.6 1.6 fusion.10
  512.3 2.7 fusion.3
  514.9 2.7 fusion.2
  517.6 0.7 constant_dynamic-slice_fusion
  (35 shorter events, 1.5 us)
Async XLA Ops:
  7.2 134.1 %all-gather.8.cloned.1.call-start = ((), (), s32[]{:S(2)}) async-start(), calls=%async_computation.1 | async-start | bytes 3684352 | tf_op jit(solution)/shard_map/all_gather | solution.py:15
  9.5 497.8 %all-reduce.3.cloned.1.call-start = ((), (), s32[]{:S(2)}) async-start(), calls=%async_computation.2 | async-start | bytes 7340032 | tf_op jit(solution)/shard_map/psum | solution.py:86
  9.6 136.2 %copy-start = (bf16[1,32,14336]{2,1,0:T(8,128)(2,1)S(1)}, bf16[1,32,14336]{2,1,0:T(8,128)(2,1)}, u32[]{:S(2)}) copy-start(bf16[1,32,14336]{2,1,0:T(8,128)(2,1)} %param.9) | copy-start | bytes 2752516
  145.7 11.9 %copy-start.1 = (bf16[1,32,14336]{2,1,0:T(8,128)(2,1)S(1)}, bf16[1,32,14336]{2,1,0:T(8,128)(2,1)}, u32[]{:S(2)}) copy-start(bf16[1,32,14336]{2,1,0:T(8,128)(2,1)} %param.10) | copy-start | bytes 2752516
  507.3 3.3 copy-start.2
Sparse Core Ops, SparseCore 0:
  13.0 128.2 all-gather.7
  210.0 297.3 all-reduce.2
